TPU v7x, 32 devices: a whole 2x2x4 slice. The times are simulated.
32 devices in a mesh: parts: 1, rows: 8 (over z, y), branch: 2 (over core), head: 2 (over x).
Axes of the slice: x: 2, y: 2, z: 4, core: 2. Of those that a mesh axis runs over, the one named last changes fastest.
Arguments:
- lineup_state: bfloat16 [32, 128, 256], P(('parts', 'rows', 'branch')), may hold values from -12 to 12
- pairwise: bfloat16 [128, 128, 128], P(('parts', 'rows', 'branch')), may hold values from -12 to 12
- aligned_residue_bounds: int32 [32, 2], P('parts'), may hold values from 0 to 128, as said below
- residue_valid_mask: int32 [128], P('parts'), may hold values from 0 to 1, as said below
- coupling_offset_weight_map: bfloat16 [128, 8], P(None, 'head'), may hold values from -0.5 to 0.5
- triangle_bias_matrix: bfloat16 [128, 4], P(None, 'head'), may hold values from -0.5 to 0.5
- alignment_projection_matrix: bfloat16 [4, 256, 256], P(None, None, 'head'), may hold values from -1 to 1
- lineup_readout_weight: bfloat16 [256, 256], replicated, may hold values from -4 to 4
- feedfwd_entry_weight: bfloat16 [256, 1024], P(None, 'head'), may hold values from -0.375 to 0.375
- feedfwd_exit_weight: bfloat16 [1024, 256], P('head'), may hold values from -0.1875 to 0.1875
- pair_projection_matrix: bfloat16 [4, 128, 128], P(None, None, 'head'), may hold values from -2 to 2
- pair_output_matrix: bfloat16 [128, 128], P(None, 'head'), may hold values from -6 to 6
- left_right_maps: bfloat16 [2, 256, 32], replicated, may hold values from -0.375 to 0.375
- outer_product_output_matrix: bfloat16 [1024, 128], P(None, 'head'), may hold values from -1.5 to 1.5
Outputs:
- refreshed_lineup_state: bfloat16 [32, 128, 256], P(('parts', 'rows', 'branch'), None, 'head')
- pairwise_out: bfloat16 [128, 128, 128], P(('parts', 'rows', 'branch'), None, 'head')
Inputs may be any that keep to these rules, and one draw needn't show every extreme that they name: `aligned_residue_bounds`: each row holds a start below its end; row 0 covers all 128 residues; every span covers a quarter of the 128 residues or more and starts in the first half. `residue_valid_mask`: 1 on a prefix that holds at least half of the 128 residues, 0 after it; the last residue is always 0.
All inputs are finite; a program needn't handle non-finite values.
Results may differ from a plain program's by a relative error of at most 0.011.
Values may be sent and summed in bfloat16 or wider, within the bound.
No kernel may reach another device: no remote copies, remote signals or barrier semaphores. Data moves between devices by JAX's collectives and lax.ppermute only.
A program may use at most 64 MiB of HBM per device.

v0:
```python
import functools
import math

import jax
import jax.numpy as jnp
from jax import lax
from jax.experimental import pallas as pl
from jax.experimental.pallas import tpu as pltpu
from jax.sharding import PartitionSpec as P


PER_FOCUS_DIM = 32
F32 = jnp.float32
BF16 = jnp.bfloat16
LOG2E = math.log2(math.e)
SCALE = LOG2E / math.sqrt(PER_FOCUS_DIM)
FAR = -1.0e30

VMEM = pl.BlockSpec(memory_space=pltpu.VMEM)
HBM = pl.BlockSpec(memory_space=pltpu.HBM)


def nt(a, b):
    return lax.dot_general(a, b, (((1,), (1,)), ((), ())), preferred_element_type=F32)


def nn(a, b):
    return lax.dot_general(a, b, (((1,), (0,)), ((), ())), preferred_element_type=F32)


def normed(values):
    values = values.astype(F32)
    center = values - jnp.mean(values, -1, keepdims=True)
    spread = jnp.mean(center * center, -1, keepdims=True)
    return center * lax.rsqrt(spread + 1e-05)


def places(shape, axis):
    return lax.broadcasted_iota(jnp.int32, shape, axis)


def place_of(cores):
    return lax.axis_index("rows") * cores + lax.axis_index("branch")


def span_of(bounds_ref, which):
    bounds = bounds_ref[...].astype(F32)
    kept = jnp.where(places(bounds.shape, 1) == which, bounds, 0.0)
    span = jnp.sum(kept, axis=1, keepdims=True)
    return span[0:1], span[1:2]


def within(at, begin, end):
    at = at.astype(F32)
    return (at >= begin) & (at < end)


def fetch(pairs, sem):
    copies = [pltpu.make_async_copy(a, b, sem.at[j]) for j, (a, b) in enumerate(pairs)]
    for copy in copies:
        copy.start()
    return copies


def pack_copies(entry_ref, exit_ref, held_ref):
    units = held_ref.shape[0]
    width = held_ref.shape[1] - units
    first = pl.multiple_of(lax.axis_index("branch") * units, units)
    begin = pl.multiple_of((1 - lax.axis_index("head")) * width, width)
    return [
        (entry_ref.at[:, pl.ds(first, units)], held_ref.at[:, pl.ds(0, units)]),
        (exit_ref.at[pl.ds(first, units), pl.ds(begin, width)], held_ref.at[:, pl.ds(units, width)]),
    ]


def pack_kernel(entry_ref, exit_ref, out_ref, sem):
    for copy in fetch(pack_copies(entry_ref, exit_ref, out_ref), sem):
        copy.wait()


def pre_kernel(cores, doubling, *refs):
    packs = []
    if len(refs) > 15 and doubling:
        entry_ref, exit_ref, packed_ref, pack_sem = refs[6], refs[7], refs[10], refs[-1]
        refs = refs[:6] + refs[8:10] + refs[11:-1]
        packs = pack_copies(entry_ref, exit_ref, packed_ref)
    if doubling:
        (near_ref, far_ref), held, in_sem = refs[6:8], refs[8:14], refs[14]
        chips = 8
    else:
        pay_ref, held, (bias_ref, factor_ref, in_sem, out_sem) = refs[6], refs[7:13], refs[13:]
        chips = pay_ref.shape[0]
    copies = fetch(list(zip(refs[:6], held)), in_sem)
    if packs:
        packs = fetch(packs, pack_sem)
    x_ref, p_ref, mb_ref, tb_ref, lr_ref, bounds_ref = held
    seqs, length, _ = x_ref.shape
    rows = p_ref.shape[0]
    depth = lr_ref.shape[1]
    first_seq = place_of(cores) * seqs
    for j in (0, 4, 5):
        copies[j].wait()
    pieces = []
    left = None
    zero = jnp.zeros(lr_ref.shape[1:], BF16)
    for s in range(seqs):
        xn = normed(x_ref[s]).astype(BF16)
        begin, end = span_of(bounds_ref, first_seq + s)
        seen = within(places((1, length), 1), begin, end)
        pieces.append(nt(lr_ref[1], xn) * seen.astype(F32))
        weight = jnp.concatenate(
            [lr_ref[0] if other == s else zero for _ in range(cores) for other in range(seqs)],
            axis=0,
        )
        term = nt(xn, weight) * within(places((length, 1), 0), begin, end).astype(F32)
        left = term if left is None else left + term
    right = jnp.concatenate(pieces, axis=0).astype(BF16)
    lanes = left.shape[1]
    group = places((rows, lanes), 1) // (seqs * depth)
    first, count = (mb_ref.shape[0] + tb_ref.shape[0]) * rows, right.shape[0]
    lefts = []
    for d in range(chips):
        mine = left[d * cores * rows : d * cores * rows + rows]
        for c in range(1, cores):
            begin = (d * cores + c) * rows
            mine = jnp.where(group == c, left[begin : begin + rows], mine)
        if lanes < length:
            mine = jnp.concatenate([mine, jnp.zeros((rows, length - lanes), F32)], axis=1)
        lefts.append(mine)
    if doubling:
        low = lax.axis_index("rows") < chips // 2
        for k, ref in enumerate((near_ref, far_ref)):
            ref[first : first + count, :] = right
            half = chips // 2
            both = [(lefts[j], lefts[half + j])[:: 1 - 2 * k] for j in range(half)]
            chosen = jnp.concatenate([jnp.where(low, x, y) for x, y in both], axis=0)
            ref[first + count : first + count + half * rows, :] = chosen.astype(BF16)
    else:
        for d in range(chips):
            factor_ref[d, 0:count, :] = right
            factor_ref[d, count : count + rows, :] = lefts[d].astype(BF16)
        sends = [pltpu.make_async_copy(factor_ref, pay_ref.at[:, first:], out_sem.at[0])]
        sends[0].start()
    for j in (1, 2, 3):
        copies[j].wait()
    bias_w = jnp.concatenate([mb_ref[...].astype(F32), tb_ref[...].astype(F32)], axis=0)
    bias_w = bias_w.astype(BF16)
    heads = bias_w.shape[0]
    biases = [nt(bias_w, normed(p_ref[i]).astype(BF16)) for i in range(rows)]
    pieces = [jnp.concatenate([b[h : h + 1] for b in biases], axis=0) for h in range(heads)]
    bias = jnp.concatenate(pieces, axis=0).astype(BF16)
    if doubling:
        near_ref[0:first, :] = bias
        far_ref[0:first, :] = bias
        for copy in packs:
            copy.wait()
        return
    for d in range(chips):
        bias_ref[d] = bias
    sends.append(pltpu.make_async_copy(bias_ref, pay_ref.at[:, 0:first], out_sem.at[1]))
    sends[1].start()
    for copy in sends:
        copy.wait()


def msa_kernel(cores, heads, rows, *refs):
    sm_ref, v_ref, g_ref, mask_ref, share_ref = refs[4:9]
    held, sem = refs[9:13], refs[13]
    copies = fetch(list(zip(refs[:4], held)), sem)
    x_ref, aw_ref, bounds_ref, valid_ref = held
    seqs, length, _ = x_ref.shape
    for copy in copies:
        copy.wait()
    first_seq = place_of(cores) * seqs
    for s in range(seqs):
        begin, end = span_of(bounds_ref, first_seq + s)
        mask_ref[s : s + 1] = jnp.where(within(places((1, length), 1), begin, end), 0.0, FAR)
    mask_ref[seqs : seqs + 1] = jnp.where(valid_ref[...] > 0, 0.0, FAR)
    begin, end = bounds_ref[0:1].astype(F32), bounds_ref[1:2].astype(F32)
    whole = within(places((length, 1), 0), begin, end).astype(BF16)
    owned = within(places((rows, 1), 0) + place_of(cores) * rows, begin, end).astype(BF16)
    share_ref[...] = 1.0 / nt(owned, whole)
    for s in range(seqs):
        xn = normed(x_ref[s]).astype(BF16)
        q = nn(xn, aw_ref[0]).astype(BF16)
        k = nn(xn, aw_ref[1]).astype(BF16)
        v_ref[s] = nn(xn, aw_ref[2]).astype(BF16)
        g_ref[s] = jax.nn.sigmoid(nn(xn, aw_ref[3]))
        head = places(q.shape, 1) // PER_FOCUS_DIM
        for h in range(heads):
            sm_ref[s, h] = nt(jnp.where(head == h, q, jnp.zeros_like(q)), k) * SCALE


def pair_kernel(pair_heads, p_ref, pw_ref, ow_ref, st_ref, pv_ref, pg_ref, own_ref, lay_ref, turn_ref, rows_ref):
    rows = p_ref.shape[0]
    width = own_ref.shape[1]
    begin = pl.multiple_of(lax.axis_index("head") * width, width)
    for i in range(rows):
        pn = normed(p_ref[i]).astype(BF16)
        q = nt(pn, pw_ref[0]).astype(BF16)
        k = nt(pn, pw_ref[1]).astype(BF16)
        pv_ref[i] = nt(pw_ref[2], pn).astype(BF16)
        pg_ref[i] = jax.nn.sigmoid(nt(pw_ref[3], pn))
        head = places(q.shape, 1) // PER_FOCUS_DIM
        for h in range(pair_heads):
            st_ref[i, h] = nt(jnp.where(head == h, q, jnp.zeros_like(q)), k) * SCALE
        turn_ref[...] = p_ref[i].astype(F32).T
        own_ref[i] = turn_ref[pl.ds(begin, width), :].astype(BF16)
    groups = 128 // width
    steps = lay_ref.shape[1] // 128
    depth = steps * groups
    turned = ow_ref[...].astype(F32)
    rows_ref[...] = jnp.concatenate([turned] * groups, axis=0).T
    group = places((depth, 128), 1) // width
    for step in range(steps):
        tile = rows_ref[pl.ds(step, depth, stride=depth), :]
        for g in range(1, groups):
            part = rows_ref[pl.ds(g * steps + step, depth, stride=depth), :]
            tile = jnp.where(group == g, part, tile)
        lay_ref[:, step * 128 : (step + 1) * 128] = tile.astype(BF16)


def sources(refs):
    core = lax.axis_index("branch")
    half = len(refs) // 2
    pairs = list(zip(refs[:half], refs[half:]))
    found = []
    if half == 1:
        for d in range(refs[0].shape[0]):
            for ref, c in zip(pairs[0], (core, 1 - core)):
                found.append((lambda lo, hi, ref=ref, d=d: ref[d, lo:hi, :], d, c))
        return found
    chip = lax.axis_index("rows")
    for e, pair in enumerate(pairs):
        count = pair[0].shape[0] // 2
        for k in range(2):
            for ref, c in zip(pair, (core, 1 - core)):
                read = lambda lo, hi, ref=ref, at=k * count: ref[at + lo : at + hi, :]
                found.append((read, chip ^ (e + 4 * k), c))
    return found


def gather_bias(bias_ref, refs, first, heads, rows, cores):
    for read, d, c in sources(refs):
        begin = pl.multiple_of((d * cores + c) * rows, rows)
        block = read(first * rows, (first + heads) * rows).astype(F32) * LOG2E
        for h in range(heads):
            bias_ref[h, pl.ds(begin, rows), :] = block[h * rows : (h + 1) * rows]


def attend(scores, values, gate):
    width = values.shape[1]
    head = places(values.shape, 1) // PER_FOCUS_DIM
    mixed = total = None
    for h, score in enumerate(scores):
        top = jnp.max(score, axis=-1, keepdims=True)
        weights = jnp.exp2(score - top).astype(BF16)
        here = head == h
        value = jnp.where(here, values, jnp.zeros_like(values))
        ones = jnp.where(here, jnp.ones_like(values), jnp.zeros_like(values))
        if width % 128 == 0:
            both = nn(weights, jnp.concatenate([value, ones], axis=1))
            part, norm = both[:, :width], both[:, width:]
        else:
            part, norm = nn(weights, value), nn(weights, ones)
        mixed = part if mixed is None else mixed + part
        total = norm if total is None else total + norm
    return gate * mixed / total


def align_kernel(cores, rows, *refs):
    gathered, (sm_ref, v_ref, g_ref, mask_ref, out_ref, bias_ref) = refs[:-6], refs[-6:]
    seqs, heads, _, _ = sm_ref.shape
    gather_bias(bias_ref, gathered, 0, heads, rows, cores)
    for s in range(seqs):
        mask = mask_ref[s : s + 1]
        scores = [sm_ref[s, h] + (bias_ref[h] + mask) for h in range(heads)]
        out_ref[s] = attend(scores, v_ref[s], g_ref[s]).astype(BF16)


def tri_kernel(cores, first, *refs):
    gathered, (st_ref, v_ref, g_ref, mask_ref, out_ref, bias_ref) = refs[:-6], refs[-6:]
    rows, heads, length, _ = st_ref.shape
    last = mask_ref.shape[0] - 1
    gather_bias(bias_ref, gathered, first, heads, rows, cores)
    for h in range(heads):
        bias_ref[h] = bias_ref[h] + mask_ref[last : last + 1]
    ones = jnp.ones((8, length), BF16)
    for i in range(rows):
        for h in range(heads):
            score = st_ref[i, h] + bias_ref[h]
            top = jnp.max(score, axis=-1, keepdims=True)
            weights = jnp.exp2(score - top).astype(BF16)
            at = slice(h * PER_FOCUS_DIM, (h + 1) * PER_FOCUS_DIM)
            mixed = nt(v_ref[i, at, :], weights)
            total = nt(ones, weights)[0:1]
            out_ref[i, at, :] = (g_ref[i, at, :] * mixed / total).astype(BF16)


def transition_kernel(parts, own_only, *refs):
    heads_refs = refs[:parts]
    x_ref, wo_ref = refs[parts : parts + 2]
    count = 1 if own_only else parts
    entry_refs = refs[parts + 2 : parts + 2 + count]
    exit_refs = refs[parts + 2 + count : parts + 2 + 2 * count]
    out_ref, turn_ref = refs[-2:]
    seqs = x_ref.shape[0]
    features = heads_refs[0].shape[2]
    width = out_ref.shape[2]
    here = lax.axis_index("head")

    def owned(value):
        if parts == 2:
            return jnp.where(here == 0, value[:, :width], value[:, width:])
        turn_ref[...] = value.T
        return turn_ref[pl.ds(pl.multiple_of(here * width, width), width), :].T

    if own_only:
        begin = pl.multiple_of(here * width, width)
        weights = [(entry_refs[0][...], exit_refs[0][:, pl.ds(begin, width)])]
        for ref in refs[-4:-2]:
            units = ref.shape[0]
            weights.append((ref[:, :units], ref[:, units:]))
    else:
        weights = [(entry[...], leave[...]) for entry, leave in zip(entry_refs, exit_refs)]
    length = x_ref.shape[1]
    for begin_row in range(0, length, 128):
        at = slice(begin_row, begin_row + 128)
        blended = jnp.concatenate([x_ref[s, at, :] for s in range(seqs)], axis=0).astype(F32)
        for j in range(parts):
            which = jnp.where(j == 0, here, 1 - here) if parts == 2 else j
            begin = pl.multiple_of(which * features, features)
            mixed = jnp.concatenate([heads_refs[j][s, at, :] for s in range(seqs)], axis=0)
            blended = blended + nn(mixed, wo_ref[pl.ds(begin, features), :])
        standardized = normed(blended).astype(BF16)
        out = owned(blended)
        for enter, leave in weights:
            value = jnp.maximum(nn(standardized, enter), 0.0).astype(BF16)
            out = out + nn(value, leave)
        for s in range(seqs):
            out_ref[s, at, :] = out[s * 128 : (s + 1) * 128].astype(BF16)


def outer_kernel(cores, seqs, heads, *refs):
    found, (w_ref, share_ref, own_ref, out_ref, a_ref, b_ref) = sources(refs[:-6]), refs[-6:]
    doubling = len(refs) > 8
    rows, width, length = out_ref.shape
    depth = w_ref.shape[0]
    lanes = depth * cores * seqs
    groups = 128 // width
    steps = depth // groups
    total = len(found) * seqs
    core = lax.axis_index("branch")
    first = heads * rows
    last = first + seqs * depth
    lane_group = places((rows, lanes), 1) // depth
    slot = lax.axis_index("rows") % 4
    for at_source, (read, _, _) in enumerate(found):
        block = read(first, last).astype(F32)
        left = read(last, last + rows)[:, :lanes].astype(F32)
        if doubling:
            every = read(last, last + 4 * rows)[:, :lanes].astype(F32)
            for k in range(1, 4):
                left = jnp.where(slot == k, every[k * rows : (k + 1) * rows], left)
        for s in range(seqs):
            row = at_source * seqs + s
            for g in range(groups):
                begin = s * depth + g * steps
                for t in range(length // 128):
                    piece = block[begin : begin + steps, t * 128 : (t + 1) * 128]
                    b_ref[g, t, pl.ds(row, steps, stride=total), :] = piece
            kept = jnp.where(lane_group == core * seqs + s, left, 0.0)
            a_ref[pl.ds(row, rows, stride=total), :] = kept
    a = a_ref[...].astype(BF16)
    share = share_ref[...]
    gathered = [[] for _ in range(rows)]
    for step in range(steps):
        tile = jnp.concatenate([w_ref[:, step * 128 : (step + 1) * 128]] * (cores * seqs), axis=0)
        g = nn(a, tile).astype(BF16)
        for i in range(rows):
            gathered[i].append(g[i * total : (i + 1) * total])
    b = [[b_ref[g, t].T.astype(BF16) for t in range(length // 128)] for g in range(groups)]
    for i in range(rows):
        g = jnp.concatenate(gathered[i], axis=0)
        for t in range(length // 128):
            acc = None
            for k in range(groups):
                part = nn(b[k][t], g).T[k * width : (k + 1) * width]
                acc = part if acc is None else acc + part
            at = slice(t * 128, (t + 1) * 128)
            out_ref[i, :, at] = acc * share[i : i + 1, at] + own_ref[i, :, at].astype(F32)


def close_kernel(parts, *refs):
    heads_refs = refs[:parts]
    opm_ref, w_ref, fresh_ref, out_ref, copy_ref, stage_ref, sem = refs[parts:]
    copies = [
        pltpu.make_async_copy(fresh_ref, copy_ref, sem.at[0]),
        pltpu.make_async_copy(stage_ref, out_ref, sem.at[1]),
    ]
    copies[0].start()
    rows = opm_ref.shape[0]
    features = heads_refs[0].shape[1]
    own = lax.axis_index("head") == 0
    weight = w_ref[...]
    if parts == 2:
        first, second = weight[:, :features].astype(F32), weight[:, features:].astype(F32)
        turned = jnp.concatenate([second, first], axis=1)
        weight = jnp.where(own, weight.astype(F32), turned).astype(BF16)
    for i in range(rows):
        every = jnp.concatenate([ref[i] for ref in heads_refs], axis=0)
        stage_ref[i] = (opm_ref[i] + nn(weight, every)).astype(BF16)
    copies[1].start()
    for copy in copies:
        copy.wait()


def call(kernel, ins, outs, scratch=(), left=(), written=(), grant=0, flops=0):
    size = sum(a.size * a.dtype.itemsize for a in ins) + sum(
        math.prod(s) * jnp.dtype(d).itemsize for s, d in outs
    )
    held = sum(a.inner_aval.size * 4 for a in scratch )
    limit = grant or min(max((size + held) * 2, 8 << 20), 60 << 20)
    run = pl.pallas_call(
        kernel,
        compiler_params=pltpu.CompilerParams(vmem_limit_bytes=limit),
        out_shape=tuple(jax.ShapeDtypeStruct(s, d) for s, d in outs),
        in_specs=[HBM if i in left else VMEM for i in range(len(ins))],
        out_specs=tuple(HBM if i in written else VMEM for i in range(len(outs))),
        scratch_shapes=list(scratch),
        cost_estimate=pl.CostEstimate(flops=flops, bytes_accessed=size, transcendentals=0),
    )
    ins = [pltpu.with_memory_space_constraint(a, pltpu.HBM) if i in left else a for i, a in enumerate(ins)]
    return run(*ins)


def held_copies(arrays):
    return [*(pltpu.VMEM(a.shape, a.dtype) for a in arrays), pltpu.SemaphoreType.DMA((len(arrays),))]


def from_heads(value):
    if lax.axis_size("head") == 2:
        return [value, lax.ppermute(value, "head", [(0, 1), (1, 0)])]
    every = lax.all_gather(value, "head", axis=0)
    return [every[j] for j in range(every.shape[0])]


def local(
    lineup_state,
    pairwise,
    aligned_residue_bounds,
    residue_valid_mask,
    coupling_offset_weight_map,
    triangle_bias_matrix,
    alignment_projection_matrix,
    lineup_readout_weight,
    feedfwd_entry_weight,
    feedfwd_exit_weight,
    pair_projection_matrix,
    pair_output_matrix,
    left_right_maps,
    outer_product_output_matrix,
):
    seqs, length, channels = lineup_state.shape
    rows, _, pair_channels = pairwise.shape
    heads = coupling_offset_weight_map.shape[1]
    pair_heads = triangle_bias_matrix.shape[1]
    every_head = heads + pair_heads
    depth = left_right_maps.shape[2]
    chips = lax.axis_size("rows")
    cores = lax.axis_size("branch")
    parts = lax.axis_size("head")
    width = outer_product_output_matrix.shape[1]
    features = heads * PER_FOCUS_DIM
    pair_features = pair_heads * PER_FOCUS_DIM
    total = chips * cores * seqs
    bounds = aligned_residue_bounds.T

    first = (
        lineup_state,
        pairwise,
        coupling_offset_weight_map.T,
        triangle_bias_matrix.T,
        jnp.swapaxes(left_right_maps, 1, 2),
        bounds,
    )
    bias_rows = every_head * rows
    right_rows = seqs * depth
    hidden = feedfwd_entry_weight.shape[1]
    swap = [(0, 1), (1, 0)]
    packing = parts == 2 and cores == 2 and hidden == cores * channels
    pack_shape = (channels, hidden // cores + channels // parts)
    if chips == 8 and cores == 2:
        shape = (bias_rows + right_rows + chips // 2 * rows, length)
        outs = [(shape, BF16), (shape, BF16)]
        scratch = held_copies(first)
        if packing:
            first = (*first, feedfwd_entry_weight, feedfwd_exit_weight)
            outs.append((pack_shape, BF16))
            scratch.append(pltpu.SemaphoreType.DMA((2,)))
        near, far, *packed = call(
            functools.partial(pre_kernel, cores, True),
            first,
            outs,
            scratch=scratch,
            left=range(len(first)),
        )
        far = lax.ppermute(far, "rows", [(i, i ^ 4) for i in range(8)])
        both = jnp.concatenate([near, far], axis=0)
        mine = [both]
        for e in range(1, 4):
            mine.append(lax.ppermute(both, "rows", [(i, i ^ e) for i in range(8)]))
        other = []
        for e in range(4):
            other.append(lax.ppermute(mine[e], "branch", swap))
    else:
        (payload,) = call(
            functools.partial(pre_kernel, cores, False),
            first,
            (((chips, bias_rows + right_rows + rows, length), BF16),),
            scratch=[
                *held_copies(first)[:-1],
                pltpu.VMEM((chips, bias_rows, length), BF16),
                pltpu.VMEM((chips, right_rows + rows, length), BF16),
                held_copies(first)[-1],
                pltpu.SemaphoreType.DMA((2,)),
            ],
            left=range(len(first)),
            written=(0,),
            grant=60 << 20,
        )
        mine = [lax.all_to_all(payload, "rows", 0, 0, tiled=True)]
        other = [lax.ppermute(mine[0], "branch", swap)]

    if packing:
        if chips != 8:
            packed = call(
                pack_kernel,
                (feedfwd_entry_weight, feedfwd_exit_weight),
                ((pack_shape, BF16),),
                scratch=[pltpu.SemaphoreType.DMA((2,))],
                left=(0, 1),
            )
        others = [lax.ppermute(packed[0], "head", [(0, 1), (1, 0)])]
        others.append(lax.ppermute(others[0], "branch", [(0, 1), (1, 0)]))
        entries, exits = [feedfwd_entry_weight], [feedfwd_exit_weight]
    else:
        entries = lax.all_gather(feedfwd_entry_weight, "head", axis=0)
        exits = lax.all_to_all(feedfwd_exit_weight, "head", 1, 0, tiled=True)
        exits = exits.reshape(parts, -1, exits.shape[1])
        entries, exits, others = list(entries), list(exits), []

    groups = 128 // width
    second = (
        lineup_state,
        alignment_projection_matrix,
        bounds,
        residue_valid_mask.reshape(1, -1),
    )
    scores, values, gate, masks, shares = call(
        functools.partial(msa_kernel, cores, heads, rows),
        second,
        (
            ((seqs, heads, length, length), F32),
            ((seqs, length, features), BF16),
            ((seqs, length, features), F32),
            ((seqs + 1, length), F32),
            ((rows, length), F32),
        ),
        scratch=held_copies(second),
        left=range(len(second)),
        flops=1 << 28,
    )
    tri_scores, tri_values, tri_gate, own_pair, outer_w = call(
        functools.partial(pair_kernel, pair_heads),
        (
            pairwise,
            jnp.swapaxes(pair_projection_matrix, 1, 2),
            outer_product_output_matrix.T,
        ),
        (
            ((rows, pair_heads, length, length), F32),
            ((rows, pair_features, length), BF16),
            ((rows, pair_features, length), F32),
            ((rows, width, length), BF16),
            ((depth, depth * width), BF16),
        ),
        scratch=[
            pltpu.VMEM((pair_channels, length), F32),
            pltpu.VMEM((depth * depth, 128), F32),
        ],
        flops=1 << 28,
    )

    (mixed,) = call(
        functools.partial(align_kernel, cores, rows),
        (*mine, *other, scores, values, gate, masks),
        (((seqs, length, features), BF16),),
        scratch=[pltpu.VMEM((heads, length, length), F32)],
        flops=1 << 28,
    )
    mixed = from_heads(mixed)
    (pair_mixed,) = call(
        functools.partial(tri_kernel, cores, heads),
        (*mine, *other, tri_scores, tri_values, tri_gate, masks),
        (((rows, pair_features, length), BF16),),
        scratch=[pltpu.VMEM((pair_heads, length, length), F32)],
        flops=1 << 28,
    )
    pair_mixed = from_heads(pair_mixed)

    own_width = channels // parts
    (fresh,) = call(
        functools.partial(transition_kernel, parts, bool(others)),
        (*mixed, lineup_state, lineup_readout_weight, *entries, *exits, *others),
        (((seqs, length, own_width), BF16),),
        scratch=[pltpu.VMEM((channels, seqs * 128), F32)],
        flops=1 << 28,
    )

    (opm,) = call(
        functools.partial(outer_kernel, cores, seqs, every_head),
        (*mine, *other, outer_w, shares, own_pair),
        (((rows, width, length), F32),),
        scratch=[
            pltpu.VMEM((rows * total, depth * cores * seqs), F32),
            pltpu.VMEM((groups, length // 128, depth // groups * total, 128), F32),
        ],
        flops=1 << 28,
    )
    pair_out, refreshed = call(
        functools.partial(close_kernel, parts),
        (*pair_mixed, opm, pair_output_matrix.T, fresh),
        (((rows, width, length), BF16), (fresh.shape, BF16)),
        scratch=[pltpu.VMEM((rows, width, length), BF16), pltpu.SemaphoreType.DMA((2,))],
        written=(0, 1),
        flops=1 << 26,
    )
    return (refreshed, jnp.swapaxes(pair_out, 1, 2))


def solution(mesh):
    in_specs = (
        P(("parts", "rows", "branch"), None, None),
        P(("parts", "rows", "branch"), None, None),
        P("parts", None),
        P("parts"),
        P(None, "head"),
        P(None, "head"),
        P(None, None, "head"),
        P(),
        P(None, "head"),
        P("head", None),
        P(None, None, "head"),
        P(None, "head"),
        P(),
        P(None, "head"),
    )
    out_specs = (
        P(("parts", "rows", "branch"), None, "head"),
        P(("parts", "rows", "branch"), None, "head"),
    )


    return jax.shard_map(local, mesh=mesh, in_specs=in_specs, out_specs=out_specs, check_vma=False)
```

profile of v0, /device:TPU:0, one launch (start us, length us, event | category | flops | bytes accessed | tf_op | source)
XLA Modules:
  0.0 30.8 jit_solution(1390245616731297254)
XLA Ops:
  0.6 2.0 %shard_map.149 = (bf16[144,128]{1,0:T(8,128)(2,1)S(1)}, bf16[144,128]{1,0:T(8,128)(2,1)S(1)}, bf16[256,384]{1,0:T(8,128)(2,1)S(1)}) custom-call(bf16[2,128,256]{2,1,0:T(8,128)(2,1)} %refs_2_.1, bf16[8,128,128]{2,1,0:T(8,128)(2,1)} %p_ref.1, bf16[4,128]{1,0:T(4,128)(2,1)} %bitcast.13, bf16[2,128]{1,0:T(2,128)(2,1)} %bitcast.16, bf16[2,32,256]{2,1,0:T(8,128)(2,1)} %bitcast.12, ...), custom_call_target="tpu_custom_call" | custom-call | bytes 1222400 | tf_op jit(solution)/shard_map/pallas_call | solution.py:434
  2.6 4.1 %collective-permute-start = (bf16[144,128]{1,0:T(8,128)(2,1)S(1)}, bf16[144,128]{1,0:T(8,128)(2,1)S(1)}, u32[]{:S(2)}, u32[]{:S(2)}) collective-permute-start(bf16[144,128]{1,0:T(8,128)(2,1)S(1)} %get-tuple-element.18), channel_id=1, source_target_pairs={{0,16},{4,20},{8,24},{12,28},{16,0},{20,4},{24,8},{28,12},{1,17},{... | collective-permute-start | bytes 110600 | tf_op jit(solution)/shard_map/ppermute | solution.py:508
  6.7 1.5 %collective-permute-start.10 = (bf16[256,384]{1,0:T(8,128)(2,1)S(1)}, bf16[256,384]{1,0:T(8,128)(2,1)S(1)}, u32[]{:S(2)}, u32[]{:S(2)}) collective-permute-start(bf16[256,384]{1,0:T(8,128)(2,1)S(1)} %get-tuple-element.29), channel_id=1, source_target_pairs={{0,1},{1,0},{2,3},{3,2},{4,5},{5,4},{6,7},{7,6},{8,9},{9,8},{10,11... | collective-permute-start | bytes 589832 | tf_op jit(solution)/shard_map/ppermute | solution.py:544
  8.2 0.8 %collective-permute-done = bf16[144,128]{1,0:T(8,128)(2,1)S(1)} collective-permute-done((bf16[144,128]{1,0:T(8,128)(2,1)S(1)}, bf16[144,128]{1,0:T(8,128)(2,1)S(1)}, u32[]{:S(2)}, u32[]{:S(2)}) %collective-permute-start) | collective-permute-done | bytes 36896 | tf_op jit(solution)/shard_map/ppermute | solution.py:508
  9.1 2.5 %collective-permute-start.3 = (bf16[288,128]{1,0:T(8,128)(2,1)S(1)}, bf16[288,128]{1,0:T(8,128)(2,1)S(1)}, u32[]{:S(2)}, u32[]{:S(2)}) collective-permute-start(bf16[288,128]{1,0:T(8,128)(2,1)S(1)} %constant_dynamic-update-slice_fusion.refs_0_), channel_id=1, source_target_pairs={{0,12},{4,8},{8,4},{12,0},{16,28},{20,24},{24,20},{28,16},{1,13},{... | collective-permute-start | bytes 221192 | tf_op jit(solution)/shard_map/ppermute | solution.py:512
  11.6 0.7 %collective-permute-start.2 = (bf16[288,128]{1,0:T(8,128)(2,1)S(1)}, bf16[288,128]{1,0:T(8,128)(2,1)S(1)}, u32[]{:S(2)}, u32[]{:S(2)}) collective-permute-start(bf16[288,128]{1,0:T(8,128)(2,1)S(1)} %constant_dynamic-update-slice_fusion.refs_0_), channel_id=1, source_target_pairs={{0,8},{4,12},{8,0},{12,4},{16,24},{20,28},{24,16},{28,20},{1,9},{5... | collective-permute-start | bytes 221192 | tf_op jit(solution)/shard_map/ppermute | solution.py:512
  12.3 0.3 collective-permute-start.1
  12.6 0.0 collective-permute-start.4
  12.6 1.8 %collective-permute-done.3.refs_3_ = bf16[288,128]{1,0:T(8,128)(2,1)S(1)} collective-permute-done((bf16[288,128]{1,0:T(8,128)(2,1)S(1)}, bf16[288,128]{1,0:T(8,128)(2,1)S(1)}, u32[]{:S(2)}, u32[]{:S(2)}) %collective-permute-start.3) | collective-permute-done | bytes 73760 | tf_op jit(solution)/shard_map/ppermute | solution.py:512
  14.4 0.0 collective-permute-start.7
  14.4 1.6 %collective-permute-done.2.refs_2_ = bf16[288,128]{1,0:T(8,128)(2,1)S(1)} collective-permute-done((bf16[288,128]{1,0:T(8,128)(2,1)S(1)}, bf16[288,128]{1,0:T(8,128)(2,1)S(1)}, u32[]{:S(2)}, u32[]{:S(2)}) %collective-permute-start.2) | collective-permute-done | bytes 73760 | tf_op jit(solution)/shard_map/ppermute | solution.py:512
  16.0 0.0 collective-permute-start.6
  16.0 0.7 %collective-permute-done.1.refs_1_ = bf16[288,128]{1,0:T(8,128)(2,1)S(1)} collective-permute-done((bf16[288,128]{1,0:T(8,128)(2,1)S(1)}, bf16[288,128]{1,0:T(8,128)(2,1)S(1)}, u32[]{:S(2)}, u32[]{:S(2)}) %collective-permute-start.1) | collective-permute-done | bytes 73760 | tf_op jit(solution)/shard_map/ppermute | solution.py:512
  16.7 0.0 collective-permute-start.5
  16.7 0.0 collective-permute-done.10.refs_6_
  16.7 0.5 %collective-permute-start.11 = (bf16[256,384]{1,0:T(8,128)(2,1)S(1)}, bf16[256,384]{1,0:T(8,128)(2,1)S(1)}, u32[]{:S(2)}, u32[]{:S(2)}) collective-permute-start(bf16[256,384]{1,0:T(8,128)(2,1)S(1)} %collective-permute-done.10.refs_6_), channel_id=1, source_target_pairs={{0,2},{2,0},{1,3},{3,1},{4,6},{6,4},{5,7},{7,5},{8,10},{10,8},{9,1... | collective-permute-start | bytes 589832 | tf_op jit(solution)/shard_map/ppermute | solution.py:545
  17.2 0.0 copy-start.3
  17.2 0.0 copy-start.6
  17.2 0.0 copy-start.7
  17.2 1.9 %shard_map.151 = (f32[2,4,128,128]{3,2,1,0:T(8,128)S(1)}, bf16[2,128,128]{2,1,0:T(8,128)(2,1)S(1)}, f32[2,128,128]{2,1,0:T(8,128)S(1)}, f32[3,128]{1,0:T(4,128)S(1)}, f32[8,128]{1,0:T(8,128)S(1)}) custom-call(bf16[2,128,256]{2,1,0:T(8,128)(2,1)} %refs_2_.1, bf16[4,256,128]{2,1,0:T(8,128)(2,1)} %refs_1_.3, s32[2,32]{1,0:T(2,128)} %bitcast.15, s32[1,128]{1,0:T(1,128)} %bitcast.18), custom_call_target="tpu_custom_call" | custom-call | flops 268435456 | bytes 1120512 | tf_op jit(solution)/shard_map/pallas_call | solution.py:434
  19.1 0.0 copy-done.3
  19.1 0.0 copy-done.6
  19.1 0.0 copy-done.7
  19.1 2.0 %shard_map.150 = (f32[8,2,128,128]{3,2,1,0:T(8,128)S(1)}, bf16[8,64,128]{2,1,0:T(8,128)(2,1)S(1)}, f32[8,64,128]{2,1,0:T(8,128)S(1)}, bf16[8,64,128]{2,1,0:T(8,128)(2,1)S(1)}, bf16[32,2048]{1,0:T(8,128)(2,1)S(1)}) custom-call(bf16[8,128,128]{2,1,0:T(8,128)(2,1)S(1)} %copy-done.3, bf16[4,64,128]{2,1,0:T(8,128)(2,1)S(1)} %bitcast.11, bf16[64,1024]{1,0:T(8,128)(2,1)S(1)} %bitcast.10), custom_call_target="tpu_custom_call" | custom-call | flops 268435456 | bytes 2162688 | tf_op jit(solution)/shard_map/pallas_call | solution.py:434
  21.1 0.0 collective-permute-done.4.refs_4_
  21.1 0.0 collective-permute-done.7.refs_7_
  21.2 0.0 collective-permute-done.6.refs_6_
  21.2 0.0 collective-permute-done.5.refs_5_
  21.2 0.8 %shard_map.152.refs_0_ = bf16[8,64,128]{2,1,0:T(8,128)(2,1)S(1)} custom-call(bf16[288,128]{1,0:T(8,128)(2,1)S(1)} %constant_dynamic-update-slice_fusion.refs_0_, bf16[288,128]{1,0:T(8,128)(2,1)S(1)} %collective-permute-done.1.refs_1_, bf16[288,128]{1,0:T(8,128)(2,1)S(1)} %collective-permute-done.2.refs_2_, ...), custom_call_target="tpu_custom_call" | custom-call | flops 268435456 | bytes 2164224 | tf_op jit(solution)/shard_map/pallas_call | solution.py:434
  21.9 1.6 %collective-permute-start.8 = (bf16[8,64,128]{2,1,0:T(8,128)(2,1)S(1)}, bf16[8,64,128]{2,1,0:T(8,128)(2,1)S(1)}, u32[]{:S(2)}, u32[]{:S(2)}) collective-permute-start(bf16[8,64,128]{2,1,0:T(8,128)(2,1)S(1)} %shard_map.152.refs_0_), channel_id=1, source_target_pairs={{0,1},{1,0},{2,3},{3,2},{4,5},{5,4},{6,7},{7,6},{8,9},{9,8},{10,11... | collective-permute-start | bytes 393224 | tf_op jit(solution)/shard_map/ppermute | solution.py:443
  23.5 0.4 %shard_map.154.refs_0_ = bf16[2,128,128]{2,1,0:T(8,128)(2,1)S(1)} custom-call(bf16[288,128]{1,0:T(8,128)(2,1)S(1)} %constant_dynamic-update-slice_fusion.refs_0_, bf16[288,128]{1,0:T(8,128)(2,1)S(1)} %collective-permute-done.1.refs_1_, bf16[288,128]{1,0:T(8,128)(2,1)S(1)} %collective-permute-done.2.refs_2_, ...), custom_call_target="tpu_custom_call" | custom-call | flops 268435456 | bytes 1377792 | tf_op jit(solution)/shard_map/pallas_call | solution.py:434
  23.9 0.6 %collective-permute-start.9 = (bf16[2,128,128]{2,1,0:T(8,128)(2,1)S(1)}, bf16[2,128,128]{2,1,0:T(8,128)(2,1)S(1)}, u32[]{:S(2)}, u32[]{:S(2)}) collective-permute-start(bf16[2,128,128]{2,1,0:T(8,128)(2,1)S(1)} %shard_map.154.refs_0_), channel_id=1, source_target_pairs={{0,1},{1,0},{2,3},{3,2},{4,5},{5,4},{6,7},{7,6},{8,9},{9,8},{10,11... | collective-permute-start | bytes 196616 | tf_op jit(solution)/shard_map/ppermute | solution.py:443
  24.5 0.0 copy-start
  24.5 0.0 copy-start.1
  24.5 0.0 copy-start.2
  24.5 0.0 copy-start.4
  24.5 1.6 %shard_map.153.refs_2_ = f32[8,64,128]{2,1,0:T(8,128)S(1)} custom-call(bf16[288,128]{1,0:T(8,128)(2,1)S(1)} %constant_dynamic-update-slice_fusion.refs_0_, bf16[288,128]{1,0:T(8,128)(2,1)S(1)} %collective-permute-done.1.refs_1_, bf16[288,128]{1,0:T(8,128)(2,1)S(1)} %collective-permute-done.2.refs_2_, bf16[288,128]{1,0:T(8,128)(2,1)S(1)} %collective-permute-done.3.refs_3_, ...), custom_call_target="tpu_custom_call" | custom-call | flops 268435456 | bytes 1118208 | tf_op jit(solution)/shard_map/pallas_call | solution.py:434
  26.1 0.0 copy-start.5
  26.1 2.7 %collective-permute-done.9.refs_1_ = bf16[2,128,128]{2,1,0:T(8,128)(2,1)S(1)} collective-permute-done((bf16[2,128,128]{2,1,0:T(8,128)(2,1)S(1)}, bf16[2,128,128]{2,1,0:T(8,128)(2,1)S(1)}, u32[]{:S(2)}, u32[]{:S(2)}) %collective-permute-start.9) | collective-permute-done | bytes 65568 | tf_op jit(solution)/shard_map/ppermute | solution.py:443
  28.8 0.0 collective-permute-done.11.refs_7_
  28.9 0.0 copy-done
  28.9 0.0 copy-done.1
  28.9 0.0 copy-done.2
  28.9 0.0 copy-done.4
  28.9 1.0 %shard_map.155.refs_4_ = bf16[2,128,128]{2,1,0:T(8,128)(2,1)S(1)} custom-call(bf16[2,128,128]{2,1,0:T(8,128)(2,1)S(1)} %shard_map.154.refs_0_, bf16[2,128,128]{2,1,0:T(8,128)(2,1)S(1)} %collective-permute-done.9.refs_1_, bf16[2,128,256]{2,1,0:T(8,128)(2,1)S(1)} %copy-done.2, bf16[256,256]{1,0:T(8,128)(2,1)S(1)} %copy-done.4, bf16[256,512]{1,0:T(8,128)(2,1)S(1)} %copy-done, ...), custom_call_target="tpu_custom_call" | custom-call | flops 268435456 | bytes 1376256 | tf_op jit(solution)/shard_map/pallas_call | solution.py:434
  29.9 0.0 collective-permute-done.8.refs_1_
  29.9 0.0 copy-done.5
  29.9 0.9 %shard_map.156 = (bf16[8,64,128]{2,1,0:T(8,128)(2,1)}, bf16[2,128,128]{2,1,0:T(8,128)(2,1)}) custom-call(bf16[8,64,128]{2,1,0:T(8,128)(2,1)S(1)} %shard_map.152.refs_0_, bf16[8,64,128]{2,1,0:T(8,128)(2,1)S(1)} %collective-permute-done.8.refs_1_, f32[8,64,128]{2,1,0:T(8,128)S(1)} %shard_map.153.refs_2_, bf16[64,128]{1,0:T(8,128)(2,1)S(1)} %bitcast.9, ...), custom_call_target="tpu_custom_call" | custom-call | flops 67108864 | bytes 802816 | tf_op jit(solution)/shard_map/pallas_call | solution.py:434
  (2 shorter events, 0.0 us)
Async XLA Ops:
  2.6 6.5 %collective-permute-start = (bf16[144,128]{1,0:T(8,128)(2,1)S(1)}, bf16[144,128]{1,0:T(8,128)(2,1)S(1)}, u32[]{:S(2)}, u32[]{:S(2)}) collective-permute-start(bf16[144,128]{1,0:T(8,128)(2,1)S(1)} %get-tuple-element.18), channel_id=1, source_target_pairs={{0,16},{4,20},{8,24},{12,28},{16,0},{20,4},{24,8},{28,12},{1,17},{... | collective-permute-start | bytes 110600 | tf_op jit(solution)/shard_map/ppermute | solution.py:508
  6.7 10.0 %collective-permute-start.10 = (bf16[256,384]{1,0:T(8,128)(2,1)S(1)}, bf16[256,384]{1,0:T(8,128)(2,1)S(1)}, u32[]{:S(2)}, u32[]{:S(2)}) collective-permute-start(bf16[256,384]{1,0:T(8,128)(2,1)S(1)} %get-tuple-element.29), channel_id=1, source_target_pairs={{0,1},{1,0},{2,3},{3,2},{4,5},{5,4},{6,7},{7,6},{8,9},{9,8},{10,11... | collective-permute-start | bytes 589832 | tf_op jit(solution)/shard_map/ppermute | solution.py:544
  9.1 5.3 %collective-permute-start.3 = (bf16[288,128]{1,0:T(8,128)(2,1)S(1)}, bf16[288,128]{1,0:T(8,128)(2,1)S(1)}, u32[]{:S(2)}, u32[]{:S(2)}) collective-permute-start(bf16[288,128]{1,0:T(8,128)(2,1)S(1)} %constant_dynamic-update-slice_fusion.refs_0_), channel_id=1, source_target_pairs={{0,12},{4,8},{8,4},{12,0},{16,28},{20,24},{24,20},{28,16},{1,13},{... | collective-permute-start | bytes 221192 | tf_op jit(solution)/shard_map/ppermute | solution.py:512
  11.6 4.4 %collective-permute-start.2 = (bf16[288,128]{1,0:T(8,128)(2,1)S(1)}, bf16[288,128]{1,0:T(8,128)(2,1)S(1)}, u32[]{:S(2)}, u32[]{:S(2)}) collective-permute-start(bf16[288,128]{1,0:T(8,128)(2,1)S(1)} %constant_dynamic-update-slice_fusion.refs_0_), channel_id=1, source_target_pairs={{0,8},{4,12},{8,0},{12,4},{16,24},{20,28},{24,16},{28,20},{1,9},{5... | collective-permute-start | bytes 221192 | tf_op jit(solution)/shard_map/ppermute | solution.py:512
  12.3 4.4 %collective-permute-start.1 = (bf16[288,128]{1,0:T(8,128)(2,1)S(1)}, bf16[288,128]{1,0:T(8,128)(2,1)S(1)}, u32[]{:S(2)}, u32[]{:S(2)}) collective-permute-start(bf16[288,128]{1,0:T(8,128)(2,1)S(1)} %constant_dynamic-update-slice_fusion.refs_0_), channel_id=1, source_target_pairs={{0,4},{4,0},{8,12},{12,8},{16,20},{20,16},{24,28},{28,24},{1,5},{5... | collective-permute-start | bytes 221192 | tf_op jit(solution)/shard_map/ppermute | solution.py:512
  12.6 8.5 %collective-permute-start.4 = (bf16[288,128]{1,0:T(8,128)(2,1)S(1)}, bf16[288,128]{1,0:T(8,128)(2,1)S(1)}, u32[]{:S(2)}, u32[]{:S(2)}) collective-permute-start(bf16[288,128]{1,0:T(8,128)(2,1)S(1)} %constant_dynamic-update-slice_fusion.refs_0_), channel_id=1, source_target_pairs={{0,2},{2,0},{1,3},{3,1},{4,6},{6,4},{5,7},{7,5},{8,10},{10,8},{9,1... | collective-permute-start | bytes 221192 | tf_op jit(solution)/shard_map/ppermute | solution.py:515
  14.4 6.8 %collective-permute-start.7 = (bf16[288,128]{1,0:T(8,128)(2,1)S(1)}, bf16[288,128]{1,0:T(8,128)(2,1)S(1)}, u32[]{:S(2)}, u32[]{:S(2)}) collective-permute-start(bf16[288,128]{1,0:T(8,128)(2,1)S(1)} %collective-permute-done.3.refs_3_), channel_id=1, source_target_pairs={{0,2},{2,0},{1,3},{3,1},{4,6},{6,4},{5,7},{7,5},{8,10},{10,8},{9,1... | collective-permute-start | bytes 221192 | tf_op jit(solution)/shard_map/ppermute | solution.py:515
  16.0 5.2 %collective-permute-start.6 = (bf16[288,128]{1,0:T(8,128)(2,1)S(1)}, bf16[288,128]{1,0:T(8,128)(2,1)S(1)}, u32[]{:S(2)}, u32[]{:S(2)}) collective-permute-start(bf16[288,128]{1,0:T(8,128)(2,1)S(1)} %collective-permute-done.2.refs_2_), channel_id=1, source_target_pairs={{0,2},{2,0},{1,3},{3,1},{4,6},{6,4},{5,7},{7,5},{8,10},{10,8},{9,1... | collective-permute-start | bytes 221192 | tf_op jit(solution)/shard_map/ppermute | solution.py:515
  16.7 4.5 %collective-permute-start.5 = (bf16[288,128]{1,0:T(8,128)(2,1)S(1)}, bf16[288,128]{1,0:T(8,128)(2,1)S(1)}, u32[]{:S(2)}, u32[]{:S(2)}) collective-permute-start(bf16[288,128]{1,0:T(8,128)(2,1)S(1)} %collective-permute-done.1.refs_1_), channel_id=1, source_target_pairs={{0,2},{2,0},{1,3},{3,1},{4,6},{6,4},{5,7},{7,5},{8,10},{10,8},{9,1... | collective-permute-start | bytes 221192 | tf_op jit(solution)/shard_map/ppermute | solution.py:515
  16.7 12.2 %collective-permute-start.11 = (bf16[256,384]{1,0:T(8,128)(2,1)S(1)}, bf16[256,384]{1,0:T(8,128)(2,1)S(1)}, u32[]{:S(2)}, u32[]{:S(2)}) collective-permute-start(bf16[256,384]{1,0:T(8,128)(2,1)S(1)} %collective-permute-done.10.refs_6_), channel_id=1, source_target_pairs={{0,2},{2,0},{1,3},{3,1},{4,6},{6,4},{5,7},{7,5},{8,10},{10,8},{9,1... | collective-permute-start | bytes 589832 | tf_op jit(solution)/shard_map/ppermute | solution.py:545
  17.2 1.9 %copy-start.3 = (bf16[8,128,128]{2,1,0:T(8,128)(2,1)S(1)}, bf16[8,128,128]{2,1,0:T(8,128)(2,1)}, u32[]{:S(2)}) copy-start(bf16[8,128,128]{2,1,0:T(8,128)(2,1)} %p_ref.1) | copy-start | bytes 786436
  17.2 1.9 %copy-start.6 = (bf16[1024,64]{0,1:T(8,128)(2,1)S(1)}, bf16[1024,64]{0,1:T(8,128)(2,1)}, u32[]{:S(2)}) copy-start(bf16[1024,64]{0,1:T(8,128)(2,1)} %param.27) | copy-start | bytes 393220
  17.2 1.9 %copy-start.7 = (bf16[4,128,64]{1,2,0:T(8,128)(2,1)S(1)}, bf16[4,128,64]{1,2,0:T(8,128)(2,1)}, u32[]{:S(2)}) copy-start(bf16[4,128,64]{1,2,0:T(8,128)(2,1)} %param.24) | copy-start | bytes 196612
  21.9 7.9 %collective-permute-start.8 = (bf16[8,64,128]{2,1,0:T(8,128)(2,1)S(1)}, bf16[8,64,128]{2,1,0:T(8,128)(2,1)S(1)}, u32[]{:S(2)}, u32[]{:S(2)}) collective-permute-start(bf16[8,64,128]{2,1,0:T(8,128)(2,1)S(1)} %shard_map.152.refs_0_), channel_id=1, source_target_pairs={{0,1},{1,0},{2,3},{3,2},{4,5},{5,4},{6,7},{7,6},{8,9},{9,8},{10,11... | collective-permute-start | bytes 393224 | tf_op jit(solution)/shard_map/ppermute | solution.py:443
  23.9 4.9 %collective-permute-start.9 = (bf16[2,128,128]{2,1,0:T(8,128)(2,1)S(1)}, bf16[2,128,128]{2,1,0:T(8,128)(2,1)S(1)}, u32[]{:S(2)}, u32[]{:S(2)}) collective-permute-start(bf16[2,128,128]{2,1,0:T(8,128)(2,1)S(1)} %shard_map.154.refs_0_), channel_id=1, source_target_pairs={{0,1},{1,0},{2,3},{3,2},{4,5},{5,4},{6,7},{7,6},{8,9},{9,8},{10,11... | collective-permute-start | bytes 196616 | tf_op jit(solution)/shard_map/ppermute | solution.py:443
  24.5 4.3 %copy-start = (bf16[256,512]{1,0:T(8,128)(2,1)S(1)}, bf16[256,512]{1,0:T(8,128)(2,1)}, u32[]{:S(2)}) copy-start(bf16[256,512]{1,0:T(8,128)(2,1)} %refs_4_.1) | copy-start | bytes 786436
  24.5 4.3 %copy-start.1 = (bf16[512,256]{1,0:T(8,128)(2,1)S(1)}, bf16[512,256]{1,0:T(8,128)(2,1)}, u32[]{:S(2)}) copy-start(bf16[512,256]{1,0:T(8,128)(2,1)} %refs_5_.1) | copy-start | bytes 786436
  24.5 4.3 %copy-start.2 = (bf16[2,128,256]{2,1,0:T(8,128)(2,1)S(1)}, bf16[2,128,256]{2,1,0:T(8,128)(2,1)}, u32[]{:S(2)}) copy-start(bf16[2,128,256]{2,1,0:T(8,128)(2,1)} %refs_2_.1) | copy-start | bytes 393220
  24.5 4.3 %copy-start.4 = (bf16[256,256]{1,0:T(8,128)(2,1)S(1)}, bf16[256,256]{1,0:T(8,128)(2,1)}, u32[]{:S(2)}) copy-start(bf16[256,256]{1,0:T(8,128)(2,1)} %refs_3_.1) | copy-start | bytes 393220
  26.1 3.7 %copy-start.5 = (bf16[128,64]{0,1:T(8,128)(2,1)S(1)}, bf16[128,64]{0,1:T(8,128)(2,1)}, u32[]{:S(2)}) copy-start(bf16[128,64]{0,1:T(8,128)(2,1)} %param.25) | copy-start | bytes 49156
where the time goes:
time: 31 us; the launch traced here: 30.8 us
  starting transfers between devices  11.8 us (38%)
  Pallas kernels  10.6 us (34%)
  waiting for transfers between devices  7.6 us (25%)
  between operations  0.79 us (3%)
    pallas_call x8, Pallas kernels, call(): return run(*ins)  10.6 us
    ppermute x1, starting transfers between devices, local(): far = lax.ppermute(far, 'rows', [(i, i ^ 4) for i in range(8)])  4.13 us
    ppermute x3, waiting for transfers between devices, local(): mine.append(lax.ppermute(both, 'rows', [(i, i ^ e) for i in range(8)]))  4.04 us
    ppermute x3, starting transfers between devices, local(): mine.append(lax.ppermute(both, 'rows', [(i, i ^ e) for i in range(8)]))  3.55 us
    ppermute x2, waiting for transfers between devices, from_heads(): return [value, lax.ppermute(value, 'head', [(0, 1), (1, 0)])]  2.7 us
    ppermute x2, starting transfers between devices, from_heads(): return [value, lax.ppermute(value, 'head', [(0, 1), (1, 0)])]  2.15 us
    ppermute x1, starting transfers between devices, local(): others = [lax.ppermute(packed[0], 'head', [(0, 1), (1, 0)])]  1.49 us
    ppermute x1, waiting for transfers between devices, local(): far = lax.ppermute(far, 'rows', [(i, i ^ 4) for i in range(8)])  0.84 us
  transfers between devices with their start and end apart: 12, of which 5 were waited for; matrix products, arithmetic and copies ran while one was open for 0% of the time, Pallas kernels for 25%

commit v1 on v0

--- a/solution.py
+++ b/solution.py
@@ -163,12 +163,19 @@
         copy.wait()
 
 
-def msa_kernel(cores, heads, rows, *refs):
-    sm_ref, v_ref, g_ref, mask_ref, share_ref = refs[4:9]
-    held, sem = refs[9:13], refs[13]
-    copies = fetch(list(zip(refs[:4], held)), sem)
-    x_ref, aw_ref, bounds_ref, valid_ref = held
+def msa_kernel(cores, heads, rows, x_ref, aw_ref, bounds_in, valid_in, *refs):
+    sm_ref, v_ref, g_ref, mask_ref, share_ref, bounds_ref, valid_ref, sem = refs
+    copies = fetch([(bounds_in, bounds_ref), (valid_in, valid_ref)], sem)
     seqs, length, _ = x_ref.shape
+    for s in range(seqs):
+        xn = normed(x_ref[s]).astype(BF16)
+        q = nn(xn, aw_ref[0]).astype(BF16)
+        k = nn(xn, aw_ref[1]).astype(BF16)
+        v_ref[s] = nn(xn, aw_ref[2]).astype(BF16)
+        g_ref[s] = jax.nn.sigmoid(nn(xn, aw_ref[3]))
+        head = places(q.shape, 1) // PER_FOCUS_DIM
+        for h in range(heads):
+            sm_ref[s, h] = nt(jnp.where(head == h, q, jnp.zeros_like(q)), k) * SCALE
     for copy in copies:
         copy.wait()
     first_seq = place_of(cores) * seqs
@@ -180,15 +187,6 @@
     whole = within(places((length, 1), 0), begin, end).astype(BF16)
     owned = within(places((rows, 1), 0) + place_of(cores) * rows, begin, end).astype(BF16)
     share_ref[...] = 1.0 / nt(owned, whole)
-    for s in range(seqs):
-        xn = normed(x_ref[s]).astype(BF16)
-        q = nn(xn, aw_ref[0]).astype(BF16)
-        k = nn(xn, aw_ref[1]).astype(BF16)
-        v_ref[s] = nn(xn, aw_ref[2]).astype(BF16)
-        g_ref[s] = jax.nn.sigmoid(nn(xn, aw_ref[3]))
-        head = places(q.shape, 1) // PER_FOCUS_DIM
-        for h in range(heads):
-            sm_ref[s, h] = nt(jnp.where(head == h, q, jnp.zeros_like(q)), k) * SCALE
 
 
 def pair_kernel(pair_heads, p_ref, pw_ref, ow_ref, st_ref, pv_ref, pg_ref, own_ref, lay_ref, turn_ref, rows_ref):
@@ -567,8 +565,8 @@
             ((seqs + 1, length), F32),
             ((rows, length), F32),
         ),
-        scratch=held_copies(second),
-        left=range(len(second)),
+        scratch=held_copies(second[2:]),
+        left=(2, 3),
         flops=1 << 28,
     )
     tri_scores, tri_values, tri_gate, own_pair, outer_w = call(

time: 31 us -> 30.7 us (level)
  Pallas kernels: 10.6 us -> 10.2 us
    pallas_call x8, Pallas kernels: 10.6 us -> 10.2 us  [call(): return run(*ins)]
  transfers between devices with their start and end apart: 12 -> 12, of which waited for: 5 -> 5; matrix products, arithmetic and copies ran while one was open for 0% -> 0% of each run, Pallas kernels for 25% -> 24%
where the time goes in v1:
time: 30.7 us; the launch traced here: 30.5 us
  starting transfers between devices  11.8 us (38%)
  Pallas kernels  10.2 us (33%)
  waiting for transfers between devices  7.61 us (25%)
  between operations  0.81 us (3%)
    pallas_call x8, Pallas kernels, call(): return run(*ins)  10.2 us
    ppermute x1, starting transfers between devices, local(): far = lax.ppermute(far, 'rows', [(i, i ^ 4) for i in range(8)])  4.13 us
    ppermute x3, waiting for transfers between devices, local(): mine.append(lax.ppermute(both, 'rows', [(i, i ^ e) for i in range(8)]))  4.04 us
    ppermute x3, starting transfers between devices, local(): mine.append(lax.ppermute(both, 'rows', [(i, i ^ e) for i in range(8)]))  3.55 us
    ppermute x2, waiting for transfers between devices, from_heads(): return [value, lax.ppermute(value, 'head', [(0, 1), (1, 0)])]  2.71 us
    ppermute x2, starting transfers between devices, from_heads(): return [value, lax.ppermute(value, 'head', [(0, 1), (1, 0)])]  2.15 us
    ppermute x1, starting transfers between devices, local(): others = [lax.ppermute(packed[0], 'head', [(0, 1), (1, 0)])]  1.49 us
    ppermute x1, waiting for transfers between devices, local(): far = lax.ppermute(far, 'rows', [(i, i ^ 4) for i in range(8)])  0.84 us
  transfers between devices with their start and end apart: 12, of which 5 were waited for; matrix products, arithmetic and copies ran while one was open for 0% of the time, Pallas kernels for 24%

profile of v1, /device:TPU:0, one launch (start us, length us, event | category | flops | bytes accessed | tf_op | source)
XLA Modules:
  0.0 30.5 jit_solution(12746735153185319368)
XLA Ops:
  0.6 0.0 copy-start.6
  0.6 2.0 %shard_map.149 = (bf16[144,128]{1,0:T(8,128)(2,1)S(1)}, bf16[144,128]{1,0:T(8,128)(2,1)S(1)}, bf16[256,384]{1,0:T(8,128)(2,1)S(1)}) custom-call(bf16[2,128,256]{2,1,0:T(8,128)(2,1)} %refs_2_.1, bf16[8,128,128]{2,1,0:T(8,128)(2,1)} %p_ref.1, bf16[4,128]{1,0:T(4,128)(2,1)} %bitcast.13, bf16[2,128]{1,0:T(2,128)(2,1)} %bitcast.16, bf16[2,32,256]{2,1,0:T(8,128)(2,1)} %bitcast.12, ...), custom_call_target="tpu_custom_call" | custom-call | bytes 1222400 | tf_op jit(solution)/shard_map/pallas_call | solution.py:432
  2.7 0.0 copy-start.2
  2.7 4.1 %collective-permute-start = (bf16[144,128]{1,0:T(8,128)(2,1)S(1)}, bf16[144,128]{1,0:T(8,128)(2,1)S(1)}, u32[]{:S(2)}, u32[]{:S(2)}) collective-permute-start(bf16[144,128]{1,0:T(8,128)(2,1)S(1)} %get-tuple-element.18), channel_id=1, source_target_pairs={{0,16},{4,20},{8,24},{12,28},{16,0},{20,4},{24,8},{28,12},{1,17},{... | collective-permute-start | bytes 110600 | tf_op jit(solution)/shard_map/ppermute | solution.py:506
  6.8 1.5 %collective-permute-start.10 = (bf16[256,384]{1,0:T(8,128)(2,1)S(1)}, bf16[256,384]{1,0:T(8,128)(2,1)S(1)}, u32[]{:S(2)}, u32[]{:S(2)}) collective-permute-start(bf16[256,384]{1,0:T(8,128)(2,1)S(1)} %get-tuple-element.29), channel_id=1, source_target_pairs={{0,1},{1,0},{2,3},{3,2},{4,5},{5,4},{6,7},{7,6},{8,9},{9,8},{10,11... | collective-permute-start | bytes 589832 | tf_op jit(solution)/shard_map/ppermute | solution.py:542
  8.3 0.8 %collective-permute-done = bf16[144,128]{1,0:T(8,128)(2,1)S(1)} collective-permute-done((bf16[144,128]{1,0:T(8,128)(2,1)S(1)}, bf16[144,128]{1,0:T(8,128)(2,1)S(1)}, u32[]{:S(2)}, u32[]{:S(2)}) %collective-permute-start) | collective-permute-done | bytes 36896 | tf_op jit(solution)/shard_map/ppermute | solution.py:506
  9.1 2.5 %collective-permute-start.3 = (bf16[288,128]{1,0:T(8,128)(2,1)S(1)}, bf16[288,128]{1,0:T(8,128)(2,1)S(1)}, u32[]{:S(2)}, u32[]{:S(2)}) collective-permute-start(bf16[288,128]{1,0:T(8,128)(2,1)S(1)} %constant_dynamic-update-slice_fusion.refs_0_), channel_id=1, source_target_pairs={{0,12},{4,8},{8,4},{12,0},{16,28},{20,24},{24,20},{28,16},{1,13},{... | collective-permute-start | bytes 221192 | tf_op jit(solution)/shard_map/ppermute | solution.py:510
  11.7 0.7 %collective-permute-start.2 = (bf16[288,128]{1,0:T(8,128)(2,1)S(1)}, bf16[288,128]{1,0:T(8,128)(2,1)S(1)}, u32[]{:S(2)}, u32[]{:S(2)}) collective-permute-start(bf16[288,128]{1,0:T(8,128)(2,1)S(1)} %constant_dynamic-update-slice_fusion.refs_0_), channel_id=1, source_target_pairs={{0,8},{4,12},{8,0},{12,4},{16,24},{20,28},{24,16},{28,20},{1,9},{5... | collective-permute-start | bytes 221192 | tf_op jit(solution)/shard_map/ppermute | solution.py:510
  12.4 0.3 collective-permute-start.1
  12.7 0.0 collective-permute-start.4
  12.7 1.8 %collective-permute-done.3.refs_3_ = bf16[288,128]{1,0:T(8,128)(2,1)S(1)} collective-permute-done((bf16[288,128]{1,0:T(8,128)(2,1)S(1)}, bf16[288,128]{1,0:T(8,128)(2,1)S(1)}, u32[]{:S(2)}, u32[]{:S(2)}) %collective-permute-start.3) | collective-permute-done | bytes 73760 | tf_op jit(solution)/shard_map/ppermute | solution.py:510
  14.4 0.0 collective-permute-start.7
  14.5 1.6 %collective-permute-done.2.refs_2_ = bf16[288,128]{1,0:T(8,128)(2,1)S(1)} collective-permute-done((bf16[288,128]{1,0:T(8,128)(2,1)S(1)}, bf16[288,128]{1,0:T(8,128)(2,1)S(1)}, u32[]{:S(2)}, u32[]{:S(2)}) %collective-permute-start.2) | collective-permute-done | bytes 73760 | tf_op jit(solution)/shard_map/ppermute | solution.py:510
  16.0 0.0 collective-permute-start.6
  16.0 0.7 %collective-permute-done.1.refs_1_ = bf16[288,128]{1,0:T(8,128)(2,1)S(1)} collective-permute-done((bf16[288,128]{1,0:T(8,128)(2,1)S(1)}, bf16[288,128]{1,0:T(8,128)(2,1)S(1)}, u32[]{:S(2)}, u32[]{:S(2)}) %collective-permute-start.1) | collective-permute-done | bytes 73760 | tf_op jit(solution)/shard_map/ppermute | solution.py:510
  16.7 0.0 collective-permute-start.5
  16.7 0.0 collective-permute-done.10.refs_6_
  16.7 0.5 %collective-permute-start.11 = (bf16[256,384]{1,0:T(8,128)(2,1)S(1)}, bf16[256,384]{1,0:T(8,128)(2,1)S(1)}, u32[]{:S(2)}, u32[]{:S(2)}) collective-permute-start(bf16[256,384]{1,0:T(8,128)(2,1)S(1)} %collective-permute-done.10.refs_6_), channel_id=1, source_target_pairs={{0,2},{2,0},{1,3},{3,1},{4,6},{6,4},{5,7},{7,5},{8,10},{10,8},{9,1... | collective-permute-start | bytes 589832 | tf_op jit(solution)/shard_map/ppermute | solution.py:543
  17.3 0.0 copy-done.6
  17.3 0.0 copy-done.2
  17.3 0.0 copy-start.3
  17.3 0.0 copy-start.7
  17.3 0.0 copy-start.8
  17.3 1.5 %shard_map.151 = (f32[2,4,128,128]{3,2,1,0:T(8,128)S(1)}, bf16[2,128,128]{2,1,0:T(8,128)(2,1)S(1)}, f32[2,128,128]{2,1,0:T(8,128)S(1)}, f32[3,128]{1,0:T(4,128)S(1)}, f32[8,128]{1,0:T(8,128)S(1)}) custom-call(bf16[2,128,256]{2,1,0:T(8,128)(2,1)S(1)} %copy-done.2, bf16[4,256,128]{2,1,0:T(8,128)(2,1)S(1)} %copy-done.6, s32[2,32]{1,0:T(2,128)} %bitcast.15, ...), custom_call_target="tpu_custom_call" | custom-call | flops 268435456 | bytes 1120512 | tf_op jit(solution)/shard_map/pallas_call | solution.py:432
  18.8 0.0 copy-done.3
  18.8 0.0 copy-done.7
  18.8 0.0 copy-done.8
  18.8 2.0 %shard_map.150 = (f32[8,2,128,128]{3,2,1,0:T(8,128)S(1)}, bf16[8,64,128]{2,1,0:T(8,128)(2,1)S(1)}, f32[8,64,128]{2,1,0:T(8,128)S(1)}, bf16[8,64,128]{2,1,0:T(8,128)(2,1)S(1)}, bf16[32,2048]{1,0:T(8,128)(2,1)S(1)}) custom-call(bf16[8,128,128]{2,1,0:T(8,128)(2,1)S(1)} %copy-done.3, bf16[4,64,128]{2,1,0:T(8,128)(2,1)S(1)} %bitcast.11, bf16[64,1024]{1,0:T(8,128)(2,1)S(1)} %bitcast.10), custom_call_target="tpu_custom_call" | custom-call | flops 268435456 | bytes 2162688 | tf_op jit(solution)/shard_map/pallas_call | solution.py:432
  20.8 0.0 collective-permute-done.4.refs_4_
  20.9 0.0 collective-permute-done.7.refs_7_
  20.9 0.0 collective-permute-done.6.refs_6_
  20.9 0.0 collective-permute-done.5.refs_5_
  20.9 0.8 %shard_map.152.refs_0_ = bf16[8,64,128]{2,1,0:T(8,128)(2,1)S(1)} custom-call(bf16[288,128]{1,0:T(8,128)(2,1)S(1)} %constant_dynamic-update-slice_fusion.refs_0_, bf16[288,128]{1,0:T(8,128)(2,1)S(1)} %collective-permute-done.1.refs_1_, bf16[288,128]{1,0:T(8,128)(2,1)S(1)} %collective-permute-done.2.refs_2_, ...), custom_call_target="tpu_custom_call" | custom-call | flops 268435456 | bytes 2164224 | tf_op jit(solution)/shard_map/pallas_call | solution.py:432
  21.7 1.6 %collective-permute-start.8 = (bf16[8,64,128]{2,1,0:T(8,128)(2,1)S(1)}, bf16[8,64,128]{2,1,0:T(8,128)(2,1)S(1)}, u32[]{:S(2)}, u32[]{:S(2)}) collective-permute-start(bf16[8,64,128]{2,1,0:T(8,128)(2,1)S(1)} %shard_map.152.refs_0_), channel_id=1, source_target_pairs={{0,1},{1,0},{2,3},{3,2},{4,5},{5,4},{6,7},{7,6},{8,9},{9,8},{10,11... | collective-permute-start | bytes 393224 | tf_op jit(solution)/shard_map/ppermute | solution.py:441
  23.2 0.4 %shard_map.154.refs_0_ = bf16[2,128,128]{2,1,0:T(8,128)(2,1)S(1)} custom-call(bf16[288,128]{1,0:T(8,128)(2,1)S(1)} %constant_dynamic-update-slice_fusion.refs_0_, bf16[288,128]{1,0:T(8,128)(2,1)S(1)} %collective-permute-done.1.refs_1_, bf16[288,128]{1,0:T(8,128)(2,1)S(1)} %collective-permute-done.2.refs_2_, ...), custom_call_target="tpu_custom_call" | custom-call | flops 268435456 | bytes 1377792 | tf_op jit(solution)/shard_map/pallas_call | solution.py:432
  23.6 0.6 %collective-permute-start.9 = (bf16[2,128,128]{2,1,0:T(8,128)(2,1)S(1)}, bf16[2,128,128]{2,1,0:T(8,128)(2,1)S(1)}, u32[]{:S(2)}, u32[]{:S(2)}) collective-permute-start(bf16[2,128,128]{2,1,0:T(8,128)(2,1)S(1)} %shard_map.154.refs_0_), channel_id=1, source_target_pairs={{0,1},{1,0},{2,3},{3,2},{4,5},{5,4},{6,7},{7,6},{8,9},{9,8},{10,11... | collective-permute-start | bytes 196616 | tf_op jit(solution)/shard_map/ppermute | solution.py:441
  24.2 0.0 copy-start
  24.2 0.0 copy-start.1
  24.2 0.0 copy-start.4
  24.2 1.6 %shard_map.153.refs_2_ = f32[8,64,128]{2,1,0:T(8,128)S(1)} custom-call(bf16[288,128]{1,0:T(8,128)(2,1)S(1)} %constant_dynamic-update-slice_fusion.refs_0_, bf16[288,128]{1,0:T(8,128)(2,1)S(1)} %collective-permute-done.1.refs_1_, bf16[288,128]{1,0:T(8,128)(2,1)S(1)} %collective-permute-done.2.refs_2_, bf16[288,128]{1,0:T(8,128)(2,1)S(1)} %collective-permute-done.3.refs_3_, ...), custom_call_target="tpu_custom_call" | custom-call | flops 268435456 | bytes 1118208 | tf_op jit(solution)/shard_map/pallas_call | solution.py:432
  25.8 0.0 copy-start.5
  25.8 2.7 %collective-permute-done.9.refs_1_ = bf16[2,128,128]{2,1,0:T(8,128)(2,1)S(1)} collective-permute-done((bf16[2,128,128]{2,1,0:T(8,128)(2,1)S(1)}, bf16[2,128,128]{2,1,0:T(8,128)(2,1)S(1)}, u32[]{:S(2)}, u32[]{:S(2)}) %collective-permute-start.9) | collective-permute-done | bytes 65568 | tf_op jit(solution)/shard_map/ppermute | solution.py:441
  28.6 0.0 collective-permute-done.11.refs_7_
  28.6 0.0 copy-done
  28.6 0.0 copy-done.1
  28.6 0.0 copy-done.4
  28.6 1.0 %shard_map.155.refs_4_ = bf16[2,128,128]{2,1,0:T(8,128)(2,1)S(1)} custom-call(bf16[2,128,128]{2,1,0:T(8,128)(2,1)S(1)} %shard_map.154.refs_0_, bf16[2,128,128]{2,1,0:T(8,128)(2,1)S(1)} %collective-permute-done.9.refs_1_, bf16[2,128,256]{2,1,0:T(8,128)(2,1)S(1)} %copy-done.2, bf16[256,256]{1,0:T(8,128)(2,1)S(1)} %copy-done.4, bf16[256,512]{1,0:T(8,128)(2,1)S(1)} %copy-done, ...), custom_call_target="tpu_custom_call" | custom-call | flops 268435456 | bytes 1376256 | tf_op jit(solution)/shard_map/pallas_call | solution.py:432
  29.6 0.0 collective-permute-done.8.refs_1_
  29.6 0.0 copy-done.5
  29.6 0.9 %shard_map.156 = (bf16[8,64,128]{2,1,0:T(8,128)(2,1)}, bf16[2,128,128]{2,1,0:T(8,128)(2,1)}) custom-call(bf16[8,64,128]{2,1,0:T(8,128)(2,1)S(1)} %shard_map.152.refs_0_, bf16[8,64,128]{2,1,0:T(8,128)(2,1)S(1)} %collective-permute-done.8.refs_1_, f32[8,64,128]{2,1,0:T(8,128)S(1)} %shard_map.153.refs_2_, bf16[64,128]{1,0:T(8,128)(2,1)S(1)} %bitcast.9, ...), custom_call_target="tpu_custom_call" | custom-call | flops 67108864 | bytes 802816 | tf_op jit(solution)/shard_map/pallas_call | solution.py:432
  (2 shorter events, 0.0 us)
Async XLA Ops:
  0.6 16.6 %copy-start.6 = (bf16[4,256,128]{2,1,0:T(8,128)(2,1)S(1)}, bf16[4,256,128]{2,1,0:T(8,128)(2,1)}, u32[]{:S(2)}) copy-start(bf16[4,256,128]{2,1,0:T(8,128)(2,1)} %aw_ref.1) | copy-start | bytes 786436
  2.7 14.6 %copy-start.2 = (bf16[2,128,256]{2,1,0:T(8,128)(2,1)S(1)}, bf16[2,128,256]{2,1,0:T(8,128)(2,1)}, u32[]{:S(2)}) copy-start(bf16[2,128,256]{2,1,0:T(8,128)(2,1)} %refs_2_.1) | copy-start | bytes 393220
  2.7 6.5 %collective-permute-start = (bf16[144,128]{1,0:T(8,128)(2,1)S(1)}, bf16[144,128]{1,0:T(8,128)(2,1)S(1)}, u32[]{:S(2)}, u32[]{:S(2)}) collective-permute-start(bf16[144,128]{1,0:T(8,128)(2,1)S(1)} %get-tuple-element.18), channel_id=1, source_target_pairs={{0,16},{4,20},{8,24},{12,28},{16,0},{20,4},{24,8},{28,12},{1,17},{... | collective-permute-start | bytes 110600 | tf_op jit(solution)/shard_map/ppermute | solution.py:506
  6.8 10.0 %collective-permute-start.10 = (bf16[256,384]{1,0:T(8,128)(2,1)S(1)}, bf16[256,384]{1,0:T(8,128)(2,1)S(1)}, u32[]{:S(2)}, u32[]{:S(2)}) collective-permute-start(bf16[256,384]{1,0:T(8,128)(2,1)S(1)} %get-tuple-element.29), channel_id=1, source_target_pairs={{0,1},{1,0},{2,3},{3,2},{4,5},{5,4},{6,7},{7,6},{8,9},{9,8},{10,11... | collective-permute-start | bytes 589832 | tf_op jit(solution)/shard_map/ppermute | solution.py:542
  9.1 5.3 %collective-permute-start.3 = (bf16[288,128]{1,0:T(8,128)(2,1)S(1)}, bf16[288,128]{1,0:T(8,128)(2,1)S(1)}, u32[]{:S(2)}, u32[]{:S(2)}) collective-permute-start(bf16[288,128]{1,0:T(8,128)(2,1)S(1)} %constant_dynamic-update-slice_fusion.refs_0_), channel_id=1, source_target_pairs={{0,12},{4,8},{8,4},{12,0},{16,28},{20,24},{24,20},{28,16},{1,13},{... | collective-permute-start | bytes 221192 | tf_op jit(solution)/shard_map/ppermute | solution.py:510
  11.7 4.4 %collective-permute-start.2 = (bf16[288,128]{1,0:T(8,128)(2,1)S(1)}, bf16[288,128]{1,0:T(8,128)(2,1)S(1)}, u32[]{:S(2)}, u32[]{:S(2)}) collective-permute-start(bf16[288,128]{1,0:T(8,128)(2,1)S(1)} %constant_dynamic-update-slice_fusion.refs_0_), channel_id=1, source_target_pairs={{0,8},{4,12},{8,0},{12,4},{16,24},{20,28},{24,16},{28,20},{1,9},{5... | collective-permute-start | bytes 221192 | tf_op jit(solution)/shard_map/ppermute | solution.py:510
  12.4 4.4 %collective-permute-start.1 = (bf16[288,128]{1,0:T(8,128)(2,1)S(1)}, bf16[288,128]{1,0:T(8,128)(2,1)S(1)}, u32[]{:S(2)}, u32[]{:S(2)}) collective-permute-start(bf16[288,128]{1,0:T(8,128)(2,1)S(1)} %constant_dynamic-update-slice_fusion.refs_0_), channel_id=1, source_target_pairs={{0,4},{4,0},{8,12},{12,8},{16,20},{20,16},{24,28},{28,24},{1,5},{5... | collective-permute-start | bytes 221192 | tf_op jit(solution)/shard_map/ppermute | solution.py:510
  12.7 8.2 %collective-permute-start.4 = (bf16[288,128]{1,0:T(8,128)(2,1)S(1)}, bf16[288,128]{1,0:T(8,128)(2,1)S(1)}, u32[]{:S(2)}, u32[]{:S(2)}) collective-permute-start(bf16[288,128]{1,0:T(8,128)(2,1)S(1)} %constant_dynamic-update-slice_fusion.refs_0_), channel_id=1, source_target_pairs={{0,2},{2,0},{1,3},{3,1},{4,6},{6,4},{5,7},{7,5},{8,10},{10,8},{9,1... | collective-permute-start | bytes 221192 | tf_op jit(solution)/shard_map/ppermute | solution.py:513
  14.4 6.4 %collective-permute-start.7 = (bf16[288,128]{1,0:T(8,128)(2,1)S(1)}, bf16[288,128]{1,0:T(8,128)(2,1)S(1)}, u32[]{:S(2)}, u32[]{:S(2)}) collective-permute-start(bf16[288,128]{1,0:T(8,128)(2,1)S(1)} %collective-permute-done.3.refs_3_), channel_id=1, source_target_pairs={{0,2},{2,0},{1,3},{3,1},{4,6},{6,4},{5,7},{7,5},{8,10},{10,8},{9,1... | collective-permute-start | bytes 221192 | tf_op jit(solution)/shard_map/ppermute | solution.py:513
  16.0 4.9 %collective-permute-start.6 = (bf16[288,128]{1,0:T(8,128)(2,1)S(1)}, bf16[288,128]{1,0:T(8,128)(2,1)S(1)}, u32[]{:S(2)}, u32[]{:S(2)}) collective-permute-start(bf16[288,128]{1,0:T(8,128)(2,1)S(1)} %collective-permute-done.2.refs_2_), channel_id=1, source_target_pairs={{0,2},{2,0},{1,3},{3,1},{4,6},{6,4},{5,7},{7,5},{8,10},{10,8},{9,1... | collective-permute-start | bytes 221192 | tf_op jit(solution)/shard_map/ppermute | solution.py:513
  16.7 4.1 %collective-permute-start.5 = (bf16[288,128]{1,0:T(8,128)(2,1)S(1)}, bf16[288,128]{1,0:T(8,128)(2,1)S(1)}, u32[]{:S(2)}, u32[]{:S(2)}) collective-permute-start(bf16[288,128]{1,0:T(8,128)(2,1)S(1)} %collective-permute-done.1.refs_1_), channel_id=1, source_target_pairs={{0,2},{2,0},{1,3},{3,1},{4,6},{6,4},{5,7},{7,5},{8,10},{10,8},{9,1... | collective-permute-start | bytes 221192 | tf_op jit(solution)/shard_map/ppermute | solution.py:513
  16.7 11.8 %collective-permute-start.11 = (bf16[256,384]{1,0:T(8,128)(2,1)S(1)}, bf16[256,384]{1,0:T(8,128)(2,1)S(1)}, u32[]{:S(2)}, u32[]{:S(2)}) collective-permute-start(bf16[256,384]{1,0:T(8,128)(2,1)S(1)} %collective-permute-done.10.refs_6_), channel_id=1, source_target_pairs={{0,2},{2,0},{1,3},{3,1},{4,6},{6,4},{5,7},{7,5},{8,10},{10,8},{9,1... | collective-permute-start | bytes 589832 | tf_op jit(solution)/shard_map/ppermute | solution.py:543
  17.3 1.5 %copy-start.3 = (bf16[8,128,128]{2,1,0:T(8,128)(2,1)S(1)}, bf16[8,128,128]{2,1,0:T(8,128)(2,1)}, u32[]{:S(2)}) copy-start(bf16[8,128,128]{2,1,0:T(8,128)(2,1)} %p_ref.1) | copy-start | bytes 786436
  17.3 1.5 %copy-start.7 = (bf16[1024,64]{0,1:T(8,128)(2,1)S(1)}, bf16[1024,64]{0,1:T(8,128)(2,1)}, u32[]{:S(2)}) copy-start(bf16[1024,64]{0,1:T(8,128)(2,1)} %param.27) | copy-start | bytes 393220
  17.3 1.5 %copy-start.8 = (bf16[4,128,64]{1,2,0:T(8,128)(2,1)S(1)}, bf16[4,128,64]{1,2,0:T(8,128)(2,1)}, u32[]{:S(2)}) copy-start(bf16[4,128,64]{1,2,0:T(8,128)(2,1)} %param.24) | copy-start | bytes 196612
  21.7 7.9 %collective-permute-start.8 = (bf16[8,64,128]{2,1,0:T(8,128)(2,1)S(1)}, bf16[8,64,128]{2,1,0:T(8,128)(2,1)S(1)}, u32[]{:S(2)}, u32[]{:S(2)}) collective-permute-start(bf16[8,64,128]{2,1,0:T(8,128)(2,1)S(1)} %shard_map.152.refs_0_), channel_id=1, source_target_pairs={{0,1},{1,0},{2,3},{3,2},{4,5},{5,4},{6,7},{7,6},{8,9},{9,8},{10,11... | collective-permute-start | bytes 393224 | tf_op jit(solution)/shard_map/ppermute | solution.py:441
  23.6 4.9 %collective-permute-start.9 = (bf16[2,128,128]{2,1,0:T(8,128)(2,1)S(1)}, bf16[2,128,128]{2,1,0:T(8,128)(2,1)S(1)}, u32[]{:S(2)}, u32[]{:S(2)}) collective-permute-start(bf16[2,128,128]{2,1,0:T(8,128)(2,1)S(1)} %shard_map.154.refs_0_), channel_id=1, source_target_pairs={{0,1},{1,0},{2,3},{3,2},{4,5},{5,4},{6,7},{7,6},{8,9},{9,8},{10,11... | collective-permute-start | bytes 196616 | tf_op jit(solution)/shard_map/ppermute | solution.py:441
  24.2 4.3 %copy-start = (bf16[256,512]{1,0:T(8,128)(2,1)S(1)}, bf16[256,512]{1,0:T(8,128)(2,1)}, u32[]{:S(2)}) copy-start(bf16[256,512]{1,0:T(8,128)(2,1)} %refs_4_.1) | copy-start | bytes 786436
  24.2 4.3 %copy-start.1 = (bf16[512,256]{1,0:T(8,128)(2,1)S(1)}, bf16[512,256]{1,0:T(8,128)(2,1)}, u32[]{:S(2)}) copy-start(bf16[512,256]{1,0:T(8,128)(2,1)} %refs_5_.1) | copy-start | bytes 786436
  24.2 4.3 %copy-start.4 = (bf16[256,256]{1,0:T(8,128)(2,1)S(1)}, bf16[256,256]{1,0:T(8,128)(2,1)}, u32[]{:S(2)}) copy-start(bf16[256,256]{1,0:T(8,128)(2,1)} %refs_3_.1) | copy-start | bytes 393220
  25.8 3.7 %copy-start.5 = (bf16[128,64]{0,1:T(8,128)(2,1)S(1)}, bf16[128,64]{0,1:T(8,128)(2,1)}, u32[]{:S(2)}) copy-start(bf16[128,64]{0,1:T(8,128)(2,1)} %param.25) | copy-start | bytes 49156
